TPU v7x, 32 devices: a whole 2x2x4 slice. The times are simulated.
32 devices in a mesh: scene: 2 (over y), seq: 4 (over z), head: 2 (over x), band: 2 (over core).
Axes of the slice: x: 2, y: 2, z: 4, core: 2. Of those that a mesh axis runs over, the one named last changes fastest.
Arguments:
- tokens: bfloat16 [8, 12, 37, 1024], P(('scene', 'seq'), ('head', 'band')), parts along dimension 0, may hold values from -6 to 6
- frame_gain: float32 [1024], replicated, may hold values from 0.5 to 1.5
- frame_qkv: bfloat16 [3, 1024, 1024], P(None, None, 'head'), may hold values from -6 to 6
- frame_out: bfloat16 [1024, 1024], P('head'), may hold values from -0.1875 to 0.1875
- global_gain: float32 [1024], replicated, may hold values from 0.5 to 1.5
- global_qkv: bfloat16 [3, 1024, 1024], P(None, None, 'head'), may hold values from -6 to 6
- global_out: bfloat16 [1024, 1024], P('head'), may hold values from -0.1875 to 0.1875
- head_gain: float32 [2048], replicated, may hold values from 0.5 to 1.5
- head_proj: bfloat16 [2048, 256], replicated, may hold values from -0.125 to 0.125
- head_bias: float32 [256], replicated, may hold values from -3 to 3
- head_conv: bfloat16 [3, 3, 256, 256], replicated, may hold values from -0.125 to 0.125
Outputs:
- blocks: bfloat16 [8, 12, 37, 1024], P(('scene', 'seq'), ('head', 'band')), parts along dimension 0
- features: bfloat16 [8, 12, 37, 256], P(('scene', 'seq'), ('head', 'band')), parts along dimension 0
There are 2 independent parts, one for each index of `scene`. A program takes and returns all parts, laid end to end along the dimension named above; an argument that names none is the same for every part. Nothing has to cross between parts.
All inputs are finite; a program needn't handle non-finite values.
Results may differ from a plain program's by a relative error of at most 0.017.
Values may be sent and summed in bfloat16 or wider, within the bound.
A program may use at most 256 MiB of HBM per device.

v0:
```python
import jax
import jax.numpy as jnp
from jax import lax
from jax.sharding import PartitionSpec as P

HD = 64


norm_eps = 1e-06
head_eps = 1e-05


def padded_2(block, sides, width):
    for axis, dim in sides:
        count = lax.axis_size(axis)
        forward = [(i, i + 1) for i in range(count - 1)]
        backward = [(target, source) for source, target in forward]
        low = lax.ppermute(
            lax.slice_in_dim(block, block.shape[dim] - width, None, axis=dim), axis, forward
        )
        high = lax.ppermute(lax.slice_in_dim(block, 0, width, axis=dim), axis, backward)
        block = jnp.concatenate([low, block, high], axis=dim)
    return block


def layer_norm(values, gain, epsilon):
    centre = values - jnp.mean(values, axis=-1, keepdims=True)
    spread = jnp.mean(centre * centre, axis=-1, keepdims=True)
    return centre * lax.rsqrt(spread + epsilon) * gain


def by_heads(matrix):
    return matrix.reshape(matrix.shape[0], matrix.shape[1] // HD, HD)


def attend_local(queries, keys_all, values_all):
    scores = jnp.einsum(
        "qhd,khd->qhk", by_heads(queries), by_heads(keys_all), preferred_element_type=jnp.float32
    ) * HD ** (-0.5)
    probs = jnp.exp(scores - jnp.max(scores, axis=-1, keepdims=True))
    mixed = jnp.einsum(
        "qhk,khd->qhd",
        probs.astype(jnp.bfloat16),
        by_heads(values_all),
        preferred_element_type=jnp.float32,
    )
    mixed = mixed / jnp.sum(probs, axis=-1)[..., None]
    return mixed.reshape(queries.shape).astype(jnp.bfloat16)


def key_step(local_rows, portion_rows):
    amount = portion_rows // local_rows
    best = 1
    for factor in range(1, amount + 1):
        if amount % factor == 0 and local_rows * factor <= max(local_rows, 1024):
            best = factor
    return local_rows * best


def fresh_carry(queries):
    heads_q = by_heads(queries)
    return (
        jnp.full(heads_q.shape[:2], -jnp.inf, jnp.float32),
        jnp.zeros(heads_q.shape[:2], jnp.float32),
        jnp.zeros(heads_q.shape, jnp.float32),
    )


def finish(carry, queries):
    return (carry[2] / carry[1][..., None]).reshape(queries.shape).astype(jnp.bfloat16)


def fold_keys(queries, carry, portions, local_rows):
    keys_in, values_in = portions
    step_rows = key_step(local_rows, keys_in.shape[0])
    heads_q = by_heads(queries)
    key_blocks = keys_in.reshape(-1, step_rows, keys_in.shape[1])
    value_blocks = values_in.reshape(-1, step_rows, values_in.shape[1])

    def absorb(states, blocks_pair):
        running_max, running_sum, weighted = states
        scores = jnp.einsum(
            "qhd,khd->qhk", heads_q, by_heads(blocks_pair[0]), preferred_element_type=jnp.float32
        ) * HD ** (-0.5)
        new_max = jnp.maximum(running_max, jnp.max(scores, axis=-1))
        decay = jnp.exp(running_max - new_max)
        probs = jnp.exp(scores - new_max[..., None])
        running_sum = running_sum * decay + jnp.sum(probs, axis=-1)
        weighted = weighted * decay[..., None] + jnp.einsum(
            "qhk,khd->qhd",
            probs.astype(jnp.bfloat16),
            by_heads(blocks_pair[1]),
            preferred_element_type=jnp.float32,
        )
        return ((new_max, running_sum, weighted), None)

    carry, ignored = lax.scan(absorb, carry, (key_blocks, value_blocks))
    return carry


def attention_block(inputs, gain, qkv_weight, out_weight, wide):
    normed = layer_norm(inputs.astype(jnp.float32), gain, norm_eps).astype(jnp.bfloat16)
    gathered = lax.all_gather(normed, "head", axis=1, tiled=True)
    flattened = gathered.reshape(-1, gathered.shape[-1])
    query_rows = jnp.dot(flattened, qkv_weight[0], preferred_element_type=jnp.float32).astype(
        jnp.bfloat16
    )
    key_rows = jnp.dot(flattened, qkv_weight[1], preferred_element_type=jnp.float32).astype(
        jnp.bfloat16
    )
    value_rows = jnp.dot(flattened, qkv_weight[2], preferred_element_type=jnp.float32).astype(
        jnp.bfloat16
    )
    if wide:
        carry = fold_keys(
            query_rows,
            fresh_carry(query_rows),
            (
                lax.all_gather(key_rows, ("seq", "band"), axis=0, tiled=True),
                lax.all_gather(value_rows, ("seq", "band"), axis=0, tiled=True),
            ),
            key_rows.shape[0],
        )
        attended = finish(carry, query_rows)
    else:
        keys_all, values_all = (
            lax.all_gather(key_rows, "band", axis=0, tiled=True),
            lax.all_gather(value_rows, "band", axis=0, tiled=True),
        )
        attended = attend_local(query_rows, keys_all, values_all)
    band_rows = inputs.shape[1] * inputs.shape[2]
    own_rows = lax.all_to_all(attended, "head", split_axis=0, concat_axis=1, tiled=True)
    branch = jnp.dot(
        own_rows,
        lax.all_gather(out_weight, "head", axis=0, tiled=True),
        preferred_element_type=jnp.float32,
    )
    merged = inputs.astype(jnp.float32).reshape(band_rows, -1) + branch
    return merged.astype(jnp.bfloat16).reshape(inputs.shape)


def on_device(
    tokens,
    frame_gain,
    frame_qkv,
    frame_out,
    global_gain,
    global_qkv,
    global_out,
    head_gain,
    head_proj,
    head_bias,
    head_conv,
):
    first = attention_block(tokens, frame_gain, frame_qkv, frame_out, False)
    second = attention_block(first, global_gain, global_qkv, global_out, True)
    band_height = tokens.shape[1]
    grid_width = tokens.shape[2]
    stacked = jnp.concatenate([first.astype(jnp.float32), second.astype(jnp.float32)], axis=-1)
    normed = layer_norm(stacked, head_gain, head_eps).astype(jnp.bfloat16)
    projected = (
        jnp.dot(
            normed.reshape(-1, stacked.shape[-1]), head_proj, preferred_element_type=jnp.float32
        )
        + head_bias
    )
    projected = projected.astype(jnp.bfloat16).reshape(
        tokens.shape[0], band_height, grid_width, head_proj.shape[1]
    )
    padded = padded_2(projected, ((("head", "band"), 1),), 1)
    padded = jnp.pad(padded, ((0, 0), (0, 0), (1, 1), (0, 0)))
    totals = jnp.zeros(projected.shape, jnp.float32)
    for offset_row in range(3):
        for offset_col in range(3):
            window = padded[
                :, offset_row : offset_row + band_height, offset_col : offset_col + grid_width
            ]
            totals = totals + jnp.einsum(
                "frcx,xy->frcy",
                window,
                head_conv[offset_row, offset_col],
                preferred_element_type=jnp.float32,
            )
    return (second, totals.astype(jnp.bfloat16))


def solution(mesh):
    return jax.shard_map(
        on_device,
        mesh=mesh,
        in_specs=(
            P(("scene", "seq"), ("head", "band"), None, None),
            P(),
            P(None, None, "head"),
            P("head", None),
            P(),
            P(None, None, "head"),
            P("head", None),
            P(),
            P(),
            P(),
            P(),
        ),
        out_specs=(
            P(("scene", "seq"), ("head", "band"), None, None),
            P(("scene", "seq"), ("head", "band"), None, None),
        ),
        check_vma=False,
    )
```

profile of v0, /device:TPU:0, one launch (start us, length us, event | category | flops | bytes accessed | tf_op | source)
XLA Modules:
  0.0 184.9 jit_solution(2766687566238518207)
XLA Ops:
  11.3 9.6 %all_gather.24 = bf16[1,6,37,1024]{3,2,0,1:T(8,128)(2,1)S(1)} all-gather(bf16[1,3,37,1024]{3,2,0,1:T(8,128)(2,1)S(1)} %multiply_convert_fusion.1), channel_id=1, replica_groups=mesh['scene'=2,'seq'=4,'head'=2,'band'=2] {'head'}, dimensions={1}, use_global_device_ids=true | all-gather | bytes 681984 | tf_op jit(solution)/shard_map/all_gather | solution.py:103
  35.2 3.4 %all-to-all-start = ((bf16[2,111,512]{2,1,0:T(8,128)(2,1)}), bf16[2,111,512]{2,1,0:T(8,128)(2,1)S(1)}, u32[]{:S(2)}, u32[]{:S(2)}) async-start(bf16[2,111,512]{2,1,0:T(8,128)(2,1)} %copy.47), calls=%async_computation | async-start | bytes 458752 | tf_op jit(solution)/shard_map/all_to_all | solution.py:132
  38.8 8.2 %all-to-all-done = bf16[2,111,512]{2,1,0:T(8,128)(2,1)S(1)} async-done(((bf16[2,111,512]{2,1,0:T(8,128)(2,1)}), bf16[2,111,512]{2,1,0:T(8,128)(2,1)S(1)}, u32[]{:S(2)}, u32[]{:S(2)}) %all-to-all-start) | async-done | bytes 227360 | tf_op jit(solution)/shard_map/all_to_all | solution.py:132
  47.8 2.1 %convert_reduce_fusion.1 = (f32[111]{0:T(128)S(1)}, bf16[111,1024]{1,0:T(8,128)(2,1)S(1)}) fusion(f32[111,1024]{1,0:T(8,128)S(1)} %reshape.316, bf16[111,1024]{1,0:T(8,128)(2,1)S(1)} %bitcast.210, bf16[1024,1024]{1,0:T(8,128)(2,1)} %all-gather.9.cloned.1.call-done), kind=kOutput, calls=%fused_computation.81 | convolution fusion | flops 233238416 | bytes 3006908 | tf_op jit(solution)/shard_map/dot_general | solution.py:133
  50.7 8.2 %all_gather.28 = bf16[1,6,37,1024]{3,2,0,1:T(8,128)(2,1)S(1)} all-gather(bf16[1,3,37,1024]{3,2,0,1:T(8,128)(2,1)S(1)} %multiply_convert_fusion), channel_id=1, replica_groups=mesh['scene'=2,'seq'=4,'head'=2,'band'=2] {'head'}, dimensions={1}, use_global_device_ids=true | all-gather | bytes 681984 | tf_op jit(solution)/shard_map/all_gather | solution.py:103
  59.0 2.3 %fusion.35 = bf16[1,222,512]{2,1,0:T(8,128)(2,1)} fusion(bf16[222,1024]{1,0:T(8,128)(2,1)S(1)} %reshape.321, bf16[3,1024,512]{2,1,0:T(8,128)(2,1)} %param.18), kind=kOutput, calls=%fused_computation.41 | convolution fusion | flops 232897536 | bytes 1730560 | tf_op jit(solution)/shard_map/dot_general | solution.py:108
  61.4 2.3 %fusion.36 = bf16[1,222,512]{2,1,0:T(8,128)(2,1)} fusion(bf16[222,1024]{1,0:T(8,128)(2,1)S(1)} %reshape.321, bf16[3,1024,512]{2,1,0:T(8,128)(2,1)} %param.18), kind=kOutput, calls=%fused_computation.42 | convolution fusion | flops 232897536 | bytes 1730560 | tf_op jit(solution)/shard_map/dot_general | solution.py:111
  66.9 21.8 %all-gather.13.cloned.1.call-done = bf16[8,222,512]{2,1,0:T(8,128)(2,1)} async-done(((bf16[1,222,512]{2,1,0:T(8,128)(2,1)}), bf16[8,222,512]{2,1,0:T(8,128)(2,1)}) %all-gather.13.cloned.1.call-update) | async-done | bytes 1818640 | tf_op jit(solution)/shard_map/all_gather | solution.py:119
  88.6 2.7 %reshape.322 = bf16[2,888,512]{2,1,0:T(8,128)(2,1)} reshape(bf16[8,222,512]{2,1,0:T(8,128)(2,1)} %all-gather.13.cloned.1.call-done) | data formatting | bytes 3637248 | tf_op jit(solution)/shard_map/reshape | solution.py:77
  91.3 25.4 %all-gather.15.cloned.1.call-done = bf16[8,222,512]{2,1,0:T(8,128)(2,1)} async-done(((bf16[1,222,512]{2,1,0:T(8,128)(2,1)}), bf16[8,222,512]{2,1,0:T(8,128)(2,1)}) %all-gather.15.cloned.1.call-update) | async-done | bytes 1818640 | tf_op jit(solution)/shard_map/all_gather | solution.py:120
  116.7 2.6 %reshape.324 = bf16[2,888,512]{2,1,0:T(8,128)(2,1)} reshape(bf16[8,222,512]{2,1,0:T(8,128)(2,1)} %all-gather.15.cloned.1.call-done) | data formatting | bytes 3637248 | tf_op jit(solution)/shard_map/reshape | solution.py:78
  119.3 36.0 %while.15 = (s32[]{:T(128)}, f32[222,8]{0,1:T(8,128)S(1)}, f32[222,8]{0,1:T(8,128)S(1)}, f32[222,8,64]{0,2,1:T(8,128)S(1)}, bf16[2,888,512]{2,1,0:T(8,128)(2,1)}...) while((s32[]{:T(128)}, f32[222,8]{0,1:T(8,128)S(1)}, ...), condition=%wide.region_9.10_spmd.clone, body=%wide.region_6.9_spmd.clone.sunk | while | flops 416701120 | bytes 29268588 | solution.py:97
  119.3 2.5 %constant_dynamic-slice_fusion.3 = (bf16[1,888,512]{2,1,0:T(8,128)(2,1)S(1)}, bf16[1,888,512]{2,1,0:T(8,128)(2,1)}) fusion(bf16[2,888,512]{2,1,0:T(8,128)(2,1)} %get-tuple-element.201, s32[]{:T(128)} %get-tuple-element.186, bf16[2,888,512]{2,1,0:T(8,128)(2,1)} %get-tuple-element.199), kind=kLoop, calls=%fused_computation.15.clone.1 | loop fusion | bytes 3637252 | tf_op jit(solution)/shard_map/while/body/jit(dynamic_index_in_dim)/dynamic_slice | solution.py:97
  123.4 4.7 %bitcast_reduce_fusion.3 = (f32[222,8]{0,1:T(8,128)S(1)}, f32[8,888,222]{1,2,0:T(8,128)}) fusion(bf16[888,8,64]{0,2,1:T(8,128)(2,1)S(1)} %bitcast.207, bf16[222,8,64]{0,2,1:T(8,128)(2,1)} %get-tuple-element.200), kind=kOutput, calls=%fused_computation.1.clone.1 | convolution fusion | flops 205019664 | bytes 7452096 | tf_op jit(solution)/shard_map/while/body/eval_jaxpr/qhd,khd->qhk/dot_general | solution.py:82
  128.1 4.1 %fusion.127 = f32[222,8]{0,1:T(8,128)S(1)} fusion(f32[8,888,222]{1,2,0:T(8,128)} %get-tuple-element.173, f32[222,8]{0,1:T(8,128)S(1)} %select_maximum_fusion.2), kind=kLoop, calls=%fused_computation.4.clone.1 | loop fusion | flops 4729488 | bytes 6322560 | tf_op jit(solution)/shard_map/while/body/eval_jaxpr/reduce_sum | solution.py:88
  132.9 4.4 %fusion.129 = f32[222,8,64]{0,2,1:T(8,128)S(1)} fusion(bf16[888,8,64]{0,2,1:T(8,128)(2,1)S(1)} %bitcast.206, f32[8,888,222]{1,2,0:T(8,128)} %get-tuple-element.173, f32[222,8]{0,1:T(8,128)S(1)} %select_maximum_fusion.2, f32[222,8,64]{0,2,1:T(8,128)S(1)} %get-tuple-element.189, f32[222,8]{0,1:T(8,128)S(1)} %get-tuple-element.176, pred[]{:T(512)S(6)} %compare.44), kind=kOutput, calls=%fused_computation.9.clone.1 | convolution fusion | flops 206939520 | bytes 8141185 | tf_op jit(solution)/shard_map/while/body/eval_jaxpr/qhk,khd->qhd/dot_general | solution.py:89
  137.3 2.5 %constant_dynamic-slice_fusion.3 = (bf16[1,888,512]{2,1,0:T(8,128)(2,1)S(1)}, bf16[1,888,512]{2,1,0:T(8,128)(2,1)}) fusion(bf16[2,888,512]{2,1,0:T(8,128)(2,1)} %get-tuple-element.201, s32[]{:T(128)} %get-tuple-element.186, bf16[2,888,512]{2,1,0:T(8,128)(2,1)} %get-tuple-element.199), kind=kLoop, calls=%fused_computation.15.clone.1 | loop fusion | bytes 3637252 | tf_op jit(solution)/shard_map/while/body/jit(dynamic_index_in_dim)/dynamic_slice | solution.py:97
  141.4 4.7 %bitcast_reduce_fusion.3 = (f32[222,8]{0,1:T(8,128)S(1)}, f32[8,888,222]{1,2,0:T(8,128)}) fusion(bf16[888,8,64]{0,2,1:T(8,128)(2,1)S(1)} %bitcast.207, bf16[222,8,64]{0,2,1:T(8,128)(2,1)} %get-tuple-element.200), kind=kOutput, calls=%fused_computation.1.clone.1 | convolution fusion | flops 205019664 | bytes 7452096 | tf_op jit(solution)/shard_map/while/body/eval_jaxpr/qhd,khd->qhk/dot_general | solution.py:82
  146.1 4.1 %fusion.127 = f32[222,8]{0,1:T(8,128)S(1)} fusion(f32[8,888,222]{1,2,0:T(8,128)} %get-tuple-element.173, f32[222,8]{0,1:T(8,128)S(1)} %select_maximum_fusion.2), kind=kLoop, calls=%fused_computation.4.clone.1 | loop fusion | flops 4729488 | bytes 6322560 | tf_op jit(solution)/shard_map/while/body/eval_jaxpr/reduce_sum | solution.py:88
  150.8 4.4 %fusion.129 = f32[222,8,64]{0,2,1:T(8,128)S(1)} fusion(bf16[888,8,64]{0,2,1:T(8,128)(2,1)S(1)} %bitcast.206, f32[8,888,222]{1,2,0:T(8,128)} %get-tuple-element.173, f32[222,8]{0,1:T(8,128)S(1)} %select_maximum_fusion.2, f32[222,8,64]{0,2,1:T(8,128)S(1)} %get-tuple-element.189, f32[222,8]{0,1:T(8,128)S(1)} %get-tuple-element.176, pred[]{:T(512)S(6)} %compare.44), kind=kOutput, calls=%fused_computation.9.clone.1 | convolution fusion | flops 206939520 | bytes 8141185 | tf_op jit(solution)/shard_map/while/body/eval_jaxpr/qhk,khd->qhd/dot_general | solution.py:89
  156.4 3.6 %all-to-all-start.1 = ((bf16[2,111,512]{2,1,0:T(8,128)(2,1)}), bf16[2,111,512]{2,1,0:T(8,128)(2,1)S(1)}, u32[]{:S(2)}, u32[]{:S(2)}) async-start(bf16[2,111,512]{2,1,0:T(8,128)(2,1)} %copy.53), calls=%async_computation.1 | async-start | bytes 458752 | tf_op jit(solution)/shard_map/all_to_all | solution.py:132
  161.8 3.7 %all-to-all-done.1 = bf16[2,111,512]{2,1,0:T(8,128)(2,1)S(1)} async-done(((bf16[2,111,512]{2,1,0:T(8,128)(2,1)}), bf16[2,111,512]{2,1,0:T(8,128)(2,1)S(1)}, u32[]{:S(2)}, u32[]{:S(2)}) %all-to-all-start.1) | async-done | bytes 227360 | tf_op jit(solution)/shard_map/all_to_all | solution.py:132
  166.0 2.9 %fusion.97 = (f32[111,1024]{1,0:T(8,128)}, bf16[111,1024]{1,0:T(8,128)(2,1)S(1)}) fusion(bf16[111,1024]{1,0:T(8,128)(2,1)S(1)} %bitcast.211, bf16[1024,1024]{1,0:T(8,128)(2,1)} %all-gather.11.cloned.1.call-done, bf16[111,1024]{1,0:T(8,128)(2,1)S(1)} %copy-done.2), kind=kOutput, calls=%fused_computation.135 | convolution fusion | flops 233238528 | bytes 3233792 | tf_op jit(solution)/shard_map/dot_general | solution.py:133
  173.8 2.3 %collective-permute-done.1 = bf16[1,1,37,256]{3,2,1,0:T(8,128)(2,1)S(1)} collective-permute-done((bf16[1,1,37,256]{3,2,1,0:T(8,128)(2,1)S(1)}, bf16[1,1,37,256]{3,2,1,0:T(8,128)(2,1)S(1)}, u32[]{:S(2)}, u32[]{:S(2)}) %collective-permute-start.1) | collective-permute-done | bytes 18976 | tf_op jit(solution)/shard_map/ppermute | solution.py:21
  (112 shorter events, 37.8 us)
Async XLA Ops:
  7.2 162.4 %copy-start = (bf16[2048,256]{1,0:T(8,128)(2,1)S(1)}, bf16[2048,256]{1,0:T(8,128)(2,1)}, u32[]{:S(2)}) copy-start(bf16[2048,256]{1,0:T(8,128)(2,1)} %param.21) | copy-start | bytes 3145732
  7.2 40.7 %all-gather.9.cloned.1.call-start = ((), (), s32[]{:S(2)}) async-start(), calls=%async_computation.2 | async-start | bytes 3145728 | tf_op jit(solution)/shard_map/all_gather | solution.py:135
  33.3 5.4 %copy-start.3 = (bf16[1,3,37,1024]{3,2,1,0:T(8,128)(2,1)S(1)}, bf16[1,3,37,1024]{3,2,1,0:T(8,128)(2,1)}, u32[]{:S(2)}) copy-start(bf16[1,3,37,1024]{3,2,1,0:T(8,128)(2,1)} %param.13) | copy-start | bytes 681988
  35.2 11.9 %all-to-all-start = ((bf16[2,111,512]{2,1,0:T(8,128)(2,1)}), bf16[2,111,512]{2,1,0:T(8,128)(2,1)S(1)}, u32[]{:S(2)}, u32[]{:S(2)}) async-start(bf16[2,111,512]{2,1,0:T(8,128)(2,1)} %copy.47), calls=%async_computation | async-start | bytes 458752 | tf_op jit(solution)/shard_map/all_to_all | solution.py:132
  38.6 50.0 %all-gather.13.cloned.1.call-start = ((), (), s32[]{:S(2)}) async-start(), calls=%async_computation.4 | async-start | bytes 2064384 | tf_op jit(solution)/shard_map/all_gather | solution.py:119
  38.7 11.7 %copy-start.8 = (f32[1024]{0:T(1024)S(1)}, f32[1024]{0:T(1024)}, u32[]{:S(2)}) copy-start(f32[1024]{0:T(1024)} %param.17) | copy-start | bytes 12292
  50.0 13.8 %copy-start.1 = (bf16[111,1024]{1,0:T(8,128)(2,1)}, bf16[111,1024]{1,0:T(8,128)(2,1)S(1)}, u32[]{:S(2)}) copy-start(bf16[111,1024]{1,0:T(8,128)(2,1)S(1)} %get-tuple-element.119) | copy-start | bytes 681988
  50.1 13.7 %copy-start.4 = (bf16[1,3,37,1024]{3,2,1,0:T(8,128)(2,1)}, bf16[1,3,37,1024]{3,2,1,0:T(8,128)(2,1)S(1)}, u32[]{:S(2)}) copy-start(bf16[1,3,37,1024]{3,2,1,0:T(8,128)(2,1)S(1)} %convert_element_type.137) | copy-start | bytes 681988
  61.3 55.3 %all-gather.15.cloned.1.call-start = ((), (), s32[]{:S(2)}) async-start(), calls=%async_computation.5 | async-start | bytes 2064384 | tf_op jit(solution)/shard_map/all_gather | solution.py:120
  63.8 102.2 %all-gather.11.cloned.1.call-start = ((), (), s32[]{:S(2)}) async-start(), calls=%async_computation.3 | async-start | bytes 3145728 | tf_op jit(solution)/shard_map/all_gather | solution.py:135
  155.3 10.7 %copy-start.2 = (bf16[111,1024]{1,0:T(8,128)(2,1)S(1)}, bf16[111,1024]{1,0:T(8,128)(2,1)}, u32[]{:S(2)}) copy-start(bf16[111,1024]{1,0:T(8,128)(2,1)} %copy-done.1) | copy-start | bytes 681988
  156.4 12.8 %copy-start.5 = (bf16[1,3,37,1024]{3,2,1,0:T(8,128)(2,1)S(1)}, bf16[1,3,37,1024]{3,2,1,0:T(8,128)(2,1)}, u32[]{:S(2)}) copy-start(bf16[1,3,37,1024]{3,2,1,0:T(8,128)(2,1)} %copy-done.4) | copy-start | bytes 681988
  156.4 9.0 %all-to-all-start.1 = ((bf16[2,111,512]{2,1,0:T(8,128)(2,1)}), bf16[2,111,512]{2,1,0:T(8,128)(2,1)S(1)}, u32[]{:S(2)}, u32[]{:S(2)}) async-start(bf16[2,111,512]{2,1,0:T(8,128)(2,1)} %copy.53), calls=%async_computation.1 | async-start | bytes 458752 | tf_op jit(solution)/shard_map/all_to_all | solution.py:132
  160.0 9.6 %copy-start.9 = (f32[2048]{0:T(1024)S(1)}, f32[2048]{0:T(1024)}, u32[]{:S(2)}) copy-start(f32[2048]{0:T(1024)} %param.20) | copy-start | bytes 24580
  160.0 9.6 %copy-start.10 = (f32[256]{0:T(256)S(1)}, f32[256]{0:T(256)}, u32[]{:S(2)}) copy-start(f32[256]{0:T(256)} %param.22) | copy-start | bytes 3076
  166.0 10.1 %copy-start.6 = (bf16[3,3,256,256]{3,2,1,0:T(8,128)(2,1)S(1)}, bf16[3,3,256,256]{3,2,1,0:T(8,128)(2,1)}, u32[]{:S(2)}) copy-start(bf16[3,3,256,256]{3,2,1,0:T(8,128)(2,1)} %param.23) | copy-start | bytes 3538948
  169.1 8.4 %copy-start.7 = (bf16[1,3,37,1024]{3,2,1,0:T(8,128)(2,1)}, bf16[1,3,37,1024]{3,2,1,0:T(8,128)(2,1)S(1)}, u32[]{:S(2)}) copy-start(bf16[1,3,37,1024]{3,2,1,0:T(8,128)(2,1)S(1)} %reshape.325) | copy-start | bytes 681988
  171.2 2.6 %collective-permute-start = (bf16[1,1,37,256]{3,2,1,0:T(8,128)(2,1)S(1)}, bf16[1,1,37,256]{3,2,1,0:T(8,128)(2,1)S(1)}, u32[]{:S(2)}, u32[]{:S(2)}) collective-permute-start(bf16[1,1,37,256]{3,2,1,0:T(8,128)(2,1)S(1)} %get-tuple-element.114), channel_id=1, source_target_pairs={{0,1},{1,2},{2,3},{4,5},{5,6},{6,7},{8,9},{9,10},{10,11},{12,13},{... | collective-permute-start | bytes 56840 | tf_op jit(solution)/shard_map/ppermute | solution.py:18
  172.5 3.6 %collective-permute-start.1 = (bf16[1,1,37,256]{3,2,1,0:T(8,128)(2,1)S(1)}, bf16[1,1,37,256]{3,2,1,0:T(8,128)(2,1)S(1)}, u32[]{:S(2)}, u32[]{:S(2)}) collective-permute-start(bf16[1,1,37,256]{3,2,1,0:T(8,128)(2,1)S(1)} %get-tuple-element.115), channel_id=1, source_target_pairs={{1,0},{2,1},{3,2},{5,4},{6,5},{7,6},{9,8},{10,9},{11,10},{13,12},{... | collective-permute-start | bytes 56840 | tf_op jit(solution)/shard_map/ppermute | solution.py:21
Sparse Core Ops, SparseCore 0:
  9.5 38.2 all-gather.8
  61.5 27.1 all-gather.12
  90.3 26.3 all-gather.14
  118.1 32.4 all-gather.10
where the time goes:
time: 188 us; the launch traced here: 185 us
  waiting for transfers between devices  62.7 us (33%)
  matrix products  39.8 us (21%)
  blocking collectives  22 us (12%)
  local copies, waits for them, and re-layouts  21 us (11%)
  other arithmetic  15 us (8%)
  between operations  14.2 us (8%)
  starting transfers between devices  9.93 us (5%)
    all_gather x1, waiting for transfers between devices, attention_block(): lax.all_gather(value_rows, ('seq', 'band'), axis=0, tiled=True)  25.4 us
    all_gather x1, waiting for transfers between devices, attention_block(): lax.all_gather(key_rows, ('seq', 'band'), axis=0, tiled=True)  21.8 us
    all_gather x2, blocking collectives, attention_block(): gathered = lax.all_gather(normed, 'head', axis=1, tiled=True)  17.8 us
    all_to_all x2, waiting for transfers between devices, attention_block(): lax.all_to_all(attended, 'head', split_axis=0, concat_axis=1, tiled=True)  11.9 us
    dot_general x2, matrix products, absorb(): jnp.einsum('qhd,khd->qhk', heads_q, by_heads(blocks_pair[0]), preferred_e...  9.42 us
    dynamic_slice x6, local copies, waits for them, and re-layouts, fold_keys(): carry, ignored = lax.scan(absorb, carry, (key_blocks, value_blocks))  9.3 us
    dot_general x2, matrix products, absorb(): jnp.einsum('qhk,khd->qhd', probs.astype(jnp.bfloat16), by_heads(blocks_pa...  8.89 us
    reduce_sum x2, other arithmetic, absorb(): running_sum = running_sum * decay + jnp.sum(probs, axis=-1)  8.21 us
  transfers between devices with their start and end apart: 8, of which 6 were waited for; matrix products, arithmetic and copies ran while one was open for 34% of the time, Pallas kernels for 0%

commit v1 on v0

--- a/solution.py
+++ b/solution.py
@@ -1,6 +1,10 @@
+import functools
+
 import jax
 import jax.numpy as jnp
 from jax import lax
+from jax.experimental import pallas as pl
+from jax.experimental.pallas import tpu as pltpu
 from jax.sharding import PartitionSpec as P
 
 HD = 64
@@ -184,9 +188,462 @@
     return (second, totals.astype(jnp.bfloat16))
 
 
+BF = jnp.bfloat16
+F32 = jnp.float32
+TILE = 16
+
+
+def up(count):
+    return -(-count // TILE) * TILE
+
+
+def mm(a, b):
+    return jnp.dot(a, b, preferred_element_type=F32)
+
+
+def swap(values):
+    return pltpu.roll(values, HD, axis=1)
+
+
+def scene_kernel(
+    seq,
+    real,
+    width,
+    tok,
+    f_gain,
+    f_qkv,
+    f_out,
+    g_gain,
+    g_qkv,
+    g_out,
+    h_gain,
+    h_proj,
+    h_bias,
+    h_conv,
+    blocks_ref,
+    feat_ref,
+    toks,
+    wf,
+    wg,
+    fo,
+    go,
+    wp,
+    wc,
+    q1,
+    k1,
+    v1,
+    att,
+    acc,
+    normed,
+    sqk,
+    sv,
+    rqk,
+    rv,
+    kk,
+    vx,
+    so,
+    ro,
+    a2,
+    r2,
+    pj,
+    halo,
+    xbuf,
+    send,
+    recv,
+    local,
+):
+    s, z = lax.axis_index("scene"), lax.axis_index("seq")
+    x, c = lax.axis_index("head"), lax.axis_index("band")
+    rows, dim = tok.shape
+    cols = wf.shape[2]
+    pairs = cols // (2 * HD)
+    frame = 4 * rows
+    half = frame // 2
+    peers = [None, (s, z, x, 1 - c), (s, z, 1 - x, c), (s, z, 1 - x, 1 - c)]
+
+    def z_peer(offset):
+        return (s, lax.rem(z + offset, seq), x, c)
+
+    started = []
+
+    def put(index, source, target, device):
+        copy = pltpu.make_async_remote_copy(
+            src_ref=source,
+            dst_ref=target,
+            send_sem=send.at[index],
+            recv_sem=recv.at[index],
+            device_id=device,
+            device_id_type=pl.DeviceIdType.MESH,
+        )
+        copy.start()
+        started.append(copy)
+        return copy
+
+    own_cols = pl.ds(pl.multiple_of(c * cols, cols), cols)
+    other_cols = pl.ds(pl.multiple_of((1 - c) * cols, cols), cols)
+    loads = [
+        pltpu.make_async_copy(f_qkv.at[:, :, own_cols], wf, local.at[0]),
+        pltpu.make_async_copy(f_out.at[own_cols], fo.at[0], local.at[1]),
+        pltpu.make_async_copy(f_out.at[other_cols], fo.at[1], local.at[2]),
+        pltpu.make_async_copy(g_qkv.at[:, :, own_cols], wg, local.at[3]),
+        pltpu.make_async_copy(g_out.at[own_cols], go.at[0], local.at[4]),
+        pltpu.make_async_copy(g_out.at[other_cols], go.at[1], local.at[5]),
+        pltpu.make_async_copy(h_proj, wp, local.at[6]),
+        pltpu.make_async_copy(h_conv, wc, local.at[7]),
+    ]
+    for load in loads:
+        load.start()
+
+    barrier = pltpu.get_barrier_semaphore()
+    everyone = peers[1:] + [z_peer(d) for d in range(1, seq)]
+    for device in everyone:
+        pl.semaphore_signal(
+            barrier, inc=1, device_id=device, device_id_type=pl.DeviceIdType.MESH
+        )
+    pl.semaphore_wait(barrier, len(everyone))
+
+    T_CORE, T_X, T_FWD, F_X, F_FWD, G_X, G_FWD = range(7)
+    A_CORE, A_X, A_FWD = 7, 7 + pairs, 7 + 2 * pairs
+    ZQ = 7 + 3 * pairs
+    ZV, ZO = ZQ + seq, ZQ + 2 * seq
+    B2 = ZQ + 3 * seq
+    HALO = B2 + 4
+
+    tok_x = put(T_X, tok, toks.at[2], peers[2])
+    tok_core = put(T_CORE, tok, toks.at[1], peers[1])
+    fo_x = put(F_X, f_out.at[own_cols], fo.at[2], peers[2])
+
+    block_row = lax.broadcasted_iota(jnp.int32, (rows, 1), 0)
+    block_valid = block_row < real
+    valid = jnp.concatenate([block_valid] * 4, axis=0)
+    low = lax.broadcasted_iota(jnp.int32, (1, 2 * HD), 1) < HD
+
+    def qkv1(slot, source):
+        n = layer_norm(source[...].astype(F32), f_gain[...], norm_eps).astype(BF)
+        at = pl.ds(slot * rows, rows)
+        q1[at, :] = (mm(n, wf[0]).astype(BF) * HD ** (-0.5)).astype(BF)
+        k1[at, :] = mm(n, wf[1]).astype(BF)
+        v1[at, :] = jnp.where(block_valid, mm(n, wf[2]), 0.0).astype(BF)
+
+    loads[0].wait()
+    qkv1(0, tok)
+    tok_core.wait_recv()
+    qkv1(1, toks.at[1])
+    tok_x.wait_recv()
+    tok_fwd = put(T_FWD, toks.at[2], toks.at[3], peers[1])
+    qkv1(2, toks.at[2])
+    tok_fwd.wait_recv()
+    qkv1(3, toks.at[3])
+
+    att_core, att_x = [], []
+    ones = jnp.where(valid, 1.0, 0.0).astype(BF)
+    for p in range(pairs):
+        at = pl.ds(p * 2 * HD, 2 * HD)
+        qp, kp, vp = q1[:, at], k1[:, at], v1[:, at]
+        outs = []
+        for keep in (low, jnp.logical_not(low)):
+            scores = lax.dot_general(
+                jnp.where(keep, qp, jnp.zeros_like(qp)),
+                kp,
+                (((1,), (1,)), ((), ())),
+                preferred_element_type=F32,
+            )
+            probs = jnp.exp(scores - jnp.max(scores, axis=-1, keepdims=True))
+            outs.append(mm(probs.astype(BF), jnp.where(keep, vp, ones)))
+        top = jnp.where(low, outs[0], outs[1])
+        bottom = swap(jnp.where(low, outs[1], outs[0]))
+        att[0, p] = (top / bottom).astype(BF)
+        att_x.append(put(A_X + p, att.at[0, p], att.at[2, p], peers[2]))
+        att_core.append(put(A_CORE + p, att.at[0, p], att.at[1, p], peers[1]))
+    go_x = put(G_X, g_out.at[own_cols], go.at[2], peers[2])
+
+    def gathered(group):
+        parts = []
+        for r in group:
+            for p in range(pairs):
+                parts.append(
+                    jnp.concatenate(
+                        [att[r, p, pl.ds((r ^ t) * rows, rows), :] for t in range(4)], axis=0
+                    )
+                )
+        return jnp.concatenate(parts, axis=1)
+
+    steps = dim // 256
+
+    def column(i):
+        return pl.ds(pl.multiple_of(i * 256, 256), 256)
+
+    for load in loads[1:3]:
+        load.wait()
+    for copy in att_core:
+        copy.wait_recv()
+    lhs_near = gathered((0, 1))
+
+    @pl.loop(0, steps)
+    def _(i):
+        at = column(i)
+        weight = jnp.concatenate([fo[0, :, at], fo[1, :, at]], axis=0)
+        base = jnp.concatenate(
+            [tok[:, at]] + [toks[r, :, at] for r in (1, 2, 3)], axis=0
+        ).astype(F32)
+        acc[:, at] = base + mm(lhs_near, weight)
+
+    fo_x.wait_recv()
+    fo_fwd = put(F_FWD, fo.at[2], fo.at[3], peers[1])
+    att_fwd = []
+    for p in range(pairs):
+        att_x[p].wait_recv()
+        att_fwd.append(put(A_FWD + p, att.at[2, p], att.at[3, p], peers[1]))
+    fo_fwd.wait_recv()
+    for copy in att_fwd:
+        copy.wait_recv()
+    lhs_far = gathered((2, 3))
+
+    @pl.loop(0, steps)
+    def _(i):
+        at = column(i)
+        weight = jnp.concatenate([fo[2, :, at], fo[3, :, at]], axis=0)
+        acc[:, at] += mm(lhs_far, weight)
+
+    for t in range(4):
+        at = pl.ds(t * rows, rows)
+        first = acc[at, :].astype(BF).astype(F32)
+        normed[at, :] = layer_norm(first, g_gain[...], norm_eps).astype(BF)
+    loads[3].wait()
+    n2 = normed[...]
+    for p in range(pairs):
+        at = pl.ds(p * 2 * HD, 2 * HD)
+        qp = (mm(n2, wg[0, :, at]).astype(BF) * HD ** (-0.5)).astype(F32)
+        kp = mm(n2, wg[1, :, at])
+        vp = jnp.where(valid, mm(n2, wg[2, :, at]), 0.0)
+        sqk[2 * p] = jnp.where(low, qp, swap(kp)).astype(BF)
+        sqk[2 * p + 1] = jnp.where(low, swap(qp), kp).astype(BF)
+        upper, under = vp[:half], vp[half:]
+        sv[2 * p] = jnp.where(low, upper, swap(under)).astype(BF)
+        sv[2 * p + 1] = jnp.where(low, swap(upper), under).astype(BF)
+
+    z_copies = []
+    for d in range(1, seq):
+        to = lax.rem(z + d, seq)
+        z_copies.append(put(ZQ + d, sqk.at[to], rqk.at[d], z_peer(d)))
+        z_copies.append(put(ZV + d, sv.at[to], rv.at[d], z_peer(d)))
+    rqk[0] = sqk[z]
+    rv[0] = sv[z]
+
+    go_x.wait_recv()
+    go_fwd = put(G_FWD, go.at[2], go.at[3], peers[1])
+
+    def arrange(d):
+        at = pl.ds(d * frame, frame)
+        kk[at, :] = swap(rqk[d].astype(F32)).astype(BF)
+        packed = rv[d].astype(F32)
+        spread = jnp.concatenate([packed, swap(packed)], axis=0)
+        vx[at, :] = jnp.where(low, spread, jnp.where(valid, 1.0, 0.0)).astype(BF)
+
+    arrange(0)
+    for d in range(1, seq):
+        z_copies[2 * d - 2].wait_recv()
+        z_copies[2 * d - 1].wait_recv()
+        arrange(d)
+
+    def back(d):
+        return pltpu.make_async_remote_copy(
+            src_ref=so.at[d],
+            dst_ref=ro.at[z],
+            send_sem=send.at[ZO + d],
+            recv_sem=recv.at[ZO + d],
+            device_id=z_peer(seq - d),
+            device_id_type=pl.DeviceIdType.MESH,
+        )
+
+    @pl.loop(1, seq + 1)
+    def _(i):
+        d = lax.rem(i, seq)
+        keys, values = kk[...], vx[...]
+        outs = []
+        for part in range(2):
+            qp = rqk[d, pl.ds(part * half, half), :]
+            scores = lax.dot_general(
+                jnp.where(low, qp, jnp.zeros_like(qp)),
+                keys,
+                (((1,), (1,)), ((), ())),
+                preferred_element_type=F32,
+            )
+            probs = jnp.exp(scores - jnp.max(scores, axis=-1, keepdims=True))
+            mixed = mm(probs.astype(BF), values)
+            outs.append(mixed / jnp.where(low, swap(mixed), 1.0))
+        so[d] = jnp.where(low, outs[0], swap(outs[1])).astype(BF)
+
+        @pl.when(d > 0)
+        def _():
+            back(d).start()
+
+    ro[z] = so[0]
+    for d in range(1, seq):
+        back(d).wait_recv()
+
+    for p in range(pairs):
+        at = pl.ds(p * 2 * HD, 2 * HD)
+        even, odd = ro[2 * p].astype(F32), ro[2 * p + 1].astype(F32)
+        a2[pl.ds(0, half), at] = jnp.where(low, even, swap(odd)).astype(BF)
+        a2[pl.ds(half, half), at] = jnp.where(low, swap(even), odd).astype(BF)
+    a2_copies = [
+        put(B2 + r, a2.at[pl.ds(r * rows, rows)], r2.at[r], peers[r]) for r in (2, 3, 1)
+    ]
+    own = pl.ds(0, rows)
+    first = acc[own, :].astype(BF).astype(F32)
+    for load in loads[4:]:
+        load.wait()
+    go_fwd.wait_recv()
+    branch = mm(a2[own, :], go[0])
+    for copy in a2_copies:
+        copy.wait_recv()
+    for r in range(1, 4):
+        branch = branch + mm(r2[r], go[r])
+    second = (first + branch).astype(BF)
+    blocks_ref[...] = second
+    stacked = jnp.concatenate([first, second.astype(F32)], axis=-1)
+    n3 = layer_norm(stacked, h_gain[...], head_eps).astype(BF)
+    pj[...] = (mm(n3, wp[...]) + h_bias[...]).astype(BF)
+
+    place = 2 * x + c
+    after = lax.rem(place + 1, 4)
+    before = lax.rem(place + 3, 4)
+
+    def frame_peer(index):
+        return (s, z, index // 2, lax.rem(index, 2))
+
+    start = (real - width) // TILE * TILE
+    slab = halo.shape[1]
+    down = put(HALO, pj.at[pl.ds(start, rows - start)], halo.at[0, pl.ds(0, rows - start)], frame_peer(after))
+    upward = put(HALO + 1, pj.at[pl.ds(0, slab)], halo.at[1], frame_peer(before))
+    base = 8
+    xbuf[...] = jnp.zeros_like(xbuf)
+    xbuf[base + width : base + width + real, :] = pj[...].astype(F32)[:real]
+    down.wait_recv()
+    upward.wait_recv()
+    skip = real - width - start
+    lower = jnp.where(place > 0, halo[0].astype(F32), 0.0)
+    upper = jnp.where(place < 3, halo[1].astype(F32), 0.0)
+    xbuf[base : base + width, :] = lower[skip : skip + width]
+    xbuf[base + width + real : base + 2 * width + real, :] = upper[:width]
+    col = lax.rem(block_row, width)
+    total = jnp.zeros(feat_ref.shape, F32)
+    for i in range(3):
+        for j in range(3):
+            first_row = base + width * i + j - 1
+            window = xbuf[first_row : first_row + rows, :]
+            if j == 0:
+                window = jnp.where(col > 0, window, 0.0)
+            if j == 2:
+                window = jnp.where(col < width - 1, window, 0.0)
+            total = total + mm(window.astype(BF), wc[3 * i + j])
+    feat_ref[...] = total.astype(BF)
+
+    for copy in started:
+        copy.wait_send()
+    for d in range(1, seq):
+        back(d).wait_send()
+
+
+def scene_program(seq, *arrays):
+    (tokens, f_gain, f_qkv, f_out, g_gain, g_qkv, g_out, h_gain, h_proj, h_bias, h_conv) = arrays
+    height, width, dim = tokens.shape[1:]
+    real = height * width
+    rows = up(real)
+    cols = f_qkv.shape[2] // 2
+    pairs = cols // (2 * HD)
+    channels = h_proj.shape[1]
+    frame = 4 * rows
+    half = frame // 2
+    flat = tokens.reshape(real, dim)
+    flat = jnp.concatenate([flat] + [flat[-1:]] * (rows - real), axis=0)
+    vmem = pl.BlockSpec(memory_space=pltpu.VMEM)
+    hbm = pl.BlockSpec(memory_space=pl.ANY)
+    start = (real - width) // TILE * TILE
+    slab = max(up(width), rows - start)
+    copies = 7 + 3 * pairs + 3 * seq + 4 + 2
+    blocks, features = pl.pallas_call(
+        functools.partial(scene_kernel, seq, real, width),
+        out_shape=(
+            jax.ShapeDtypeStruct((rows, dim), BF),
+            jax.ShapeDtypeStruct((rows, channels), BF),
+        ),
+        in_specs=[vmem, vmem, hbm, hbm, vmem, hbm, hbm, vmem, hbm, vmem, hbm],
+        out_specs=(vmem, vmem),
+        scratch_shapes=[
+            pltpu.VMEM((4, rows, dim), BF),
+            pltpu.VMEM((3, dim, cols), BF),
+            pltpu.VMEM((3, dim, cols), BF),
+            pltpu.VMEM((4, cols, dim), BF),
+            pltpu.VMEM((4, cols, dim), BF),
+            pltpu.VMEM(h_proj.shape, BF),
+            pltpu.VMEM((9, channels, channels), BF),
+            pltpu.VMEM((frame, cols), BF),
+            pltpu.VMEM((frame, cols), BF),
+            pltpu.VMEM((frame, cols), BF),
+            pltpu.VMEM((4, pairs, frame, 2 * HD), BF),
+            pltpu.VMEM((frame, dim), F32),
+            pltpu.VMEM((frame, dim), BF),
+            pltpu.VMEM((seq, frame, 2 * HD), BF),
+            pltpu.VMEM((seq, half, 2 * HD), BF),
+            pltpu.VMEM((seq, frame, 2 * HD), BF),
+            pltpu.VMEM((seq, half, 2 * HD), BF),
+            pltpu.VMEM((seq * frame, 2 * HD), BF),
+            pltpu.VMEM((seq * frame, 2 * HD), BF),
+            pltpu.VMEM((seq, half, 2 * HD), BF),
+            pltpu.VMEM((seq, half, 2 * HD), BF),
+            pltpu.VMEM((frame, cols), BF),
+            pltpu.VMEM((4, rows, cols), BF),
+            pltpu.VMEM((rows, channels), BF),
+            pltpu.VMEM((2, slab, channels), BF),
+            pltpu.VMEM((up(rows + 2 * width + 2 * TILE), channels), F32),
+            pltpu.SemaphoreType.DMA((copies,)),
+            pltpu.SemaphoreType.DMA((copies,)),
+            pltpu.SemaphoreType.DMA((8,)),
+        ],
+        compiler_params=pltpu.CompilerParams(
+            collective_id=0, has_side_effects=True, vmem_limit_bytes=48 * 2**20
+        ),
+    )(
+        flat,
+        f_gain.reshape(1, -1),
+        f_qkv,
+        f_out,
+        g_gain.reshape(1, -1),
+        g_qkv,
+        g_out,
+        h_gain.reshape(1, -1),
+        h_proj,
+        h_bias.reshape(1, -1),
+        h_conv.reshape(9, channels, channels),
+    )
+    return (
+        blocks[:real].reshape(tokens.shape),
+        features[:real].reshape(1, height, width, channels),
+    )
+
+
+def routed(mesh, *arrays):
+    sizes = mesh.shape
+    frames, height, width = arrays[0].shape[:3]
+    heads = arrays[2].shape[2] // HD
+    fits = (
+        sizes["head"] == 2
+        and sizes["band"] == 2
+        and frames == 1
+        and heads == 2 * sizes["seq"]
+        and sizes["seq"] % 2 == 0
+        and height * width >= up(width)
+    )
+    if fits:
+        return scene_program(sizes["seq"], *arrays)
+    return on_device(*arrays)
+
+
 def solution(mesh):
     return jax.shard_map(
-        on_device,
+        functools.partial(routed, mesh),
         mesh=mesh,
         in_specs=(
             P(("scene", "seq"), ("head", "band"), None, None),

time: 188 us -> 78.8 us (0.42); the launches traced: 185 us -> 78.4 us
  Pallas kernels: 0 us -> 67.6 us
  waiting for transfers between devices: 62.7 us -> 0 us
  matrix products: 39.8 us -> 0 us
  blocking collectives: 22 us -> 0 us
  other arithmetic: 15 us -> 0.02 us
  between operations: 14.2 us -> 0.67 us
  local copies, waits for them, and re-layouts: 21 us -> 10.1 us
  starting transfers between devices: 9.93 us -> 0 us
    pallas_call x0 -> x1, Pallas kernels: none -> 67.6 us  [scene_program(): pl.pallas_call(functools.partial(scene_kernel, seq, real, width), out_sha...]
    all_gather x4 -> x0, waiting for transfers between devices: 47.4 us -> none  [the longest x1 25.4 us: attention_block(): lax.all_gather(value_rows, ('seq', 'band'), axis=0, tiled=True)]
    dot_general x24 -> x0, matrix products: 39.8 us -> none  [the longest x2 9.42 us: absorb(): jnp.einsum('qhd,khd->qhk', heads_q, by_heads(blocks_pair[0]), preferred_e...]
    all_gather x4 -> x0, blocking collectives: 22 us -> none  [the longest x2 17.8 us: attention_block(): gathered = lax.all_gather(normed, 'head', axis=1, tiled=True)]
    all_to_all x2 -> x0, waiting for transfers between devices: 11.9 us -> none  [attention_block(): lax.all_to_all(attended, 'head', split_axis=0, concat_axis=1, tiled=True)]
    reduce_sum x8 -> x0, other arithmetic: 11.7 us -> none  [the longest x2 8.21 us: absorb(): running_sum = running_sum * decay + jnp.sum(probs, axis=-1)]
    dynamic_slice x6 -> x0, local copies, waits for them, and re-layouts: 9.3 us -> none  [fold_keys(): carry, ignored = lax.scan(absorb, carry, (key_blocks, value_blocks))]
    unnamed x26 -> x16, local copies, waits for them, and re-layouts: 0.48 us -> 7.69 us
  transfers between devices with their start and end apart: 8 -> 0, of which waited for: 6 -> 0; matrix products, arithmetic and copies ran while one was open for 34% -> 0% of each run, Pallas kernels for 0% -> 0%
where the time goes in v1:
time: 78.8 us; the launch traced here: 78.4 us
  Pallas kernels  67.6 us (86%)
  local copies, waits for them, and re-layouts  10.1 us (13%)
    pallas_call x1, Pallas kernels, scene_program(): pl.pallas_call(functools.partial(scene_kernel, seq, real, width), out_sha...  67.6 us
    unnamed x16, local copies, waits for them, and re-layouts  7.69 us

profile of v1, /device:TPU:0, one launch (start us, length us, event | category | flops | bytes accessed | tf_op | source)
XLA Modules:
  0.0 78.4 jit_solution(2734654749180610021)
XLA Ops:
  0.6 1.0 %reshape.28 = bf16[111,1024]{1,0:T(8,128)(2,1)S(1)} reshape(bf16[1,3,37,1024]{3,2,1,0:T(8,128)(2,1)} %param.11) | data formatting | bytes 454656 | tf_op jit(solution)/shard_map/reshape | solution.py:559
  1.7 0.0 copy-start
  1.7 1.3 %copy-done = bf16[3,3,256,256]{3,2,1,0:T(8,128)(2,1)S(1)} copy-done((bf16[3,3,256,256]{3,2,1,0:T(8,128)(2,1)S(1)}, bf16[3,3,256,256]{3,2,1,0:T(8,128)(2,1)}, u32[]{:S(2)}) %copy-start) | copy-done | bytes 1179672
  3.0 0.0 copy-start.1
  3.0 1.2 %copy-done.1 = bf16[512,1024]{1,0:T(8,128)(2,1)S(1)} copy-done((bf16[512,1024]{1,0:T(8,128)(2,1)S(1)}, bf16[512,1024]{1,0:T(8,128)(2,1)}, u32[]{:S(2)}) %copy-start.1) | copy-done | bytes 1048600
  4.2 0.0 copy-start.2
  4.2 1.2 %copy-done.2 = bf16[512,1024]{1,0:T(8,128)(2,1)S(1)} copy-done((bf16[512,1024]{1,0:T(8,128)(2,1)S(1)}, bf16[512,1024]{1,0:T(8,128)(2,1)}, u32[]{:S(2)}) %copy-start.2) | copy-done | bytes 1048600
  5.4 0.0 copy-start.3
  5.4 1.2 %copy-done.3 = bf16[2048,256]{1,0:T(8,128)(2,1)S(1)} copy-done((bf16[2048,256]{1,0:T(8,128)(2,1)S(1)}, bf16[2048,256]{1,0:T(8,128)(2,1)}, u32[]{:S(2)}) %copy-start.3) | copy-done | bytes 1048600
  6.6 0.0 copy-start.4
  6.6 0.7 copy-done.4
  7.3 0.0 copy-start.5
  7.3 0.7 copy-done.5
  8.0 0.0 copy-start.6
  8.0 0.7 copy-done.6
  8.7 0.0 copy-start.7
  8.7 0.7 copy-done.7
  9.4 67.6 %shard_map.122 = (bf16[112,1024]{1,0:T(8,128)(2,1)S(1)}, bf16[112,256]{1,0:T(8,128)(2,1)S(1)}) custom-call(bf16[112,1024]{1,0:T(8,128)(2,1)S(1)} %pad_maximum_fusion.tok, f32[1,1024]{1,0:T(1,128)S(1)} %bitcast.11, bf16[3,1024,512]{2,1,0:T(8,128)(2,1)} %f_qkv.1, bf16[512,1024]{1,0:T(8,128)(2,1)S(1)} %copy-done.1, f32[1,1024]{1,0:T(1,128)S(1)} %bitcast.12, ...), custom_call_target="tpu_custom_call" | custom-call | tf_op jit(solution)/shard_map/pallas_call | solution.py:566
  77.0 0.8 reshape.34
  77.7 0.6 reshape.35
  (2 shorter events, 0.0 us)
Async XLA Ops:
  1.7 1.3 %copy-start = (bf16[3,3,256,256]{3,2,1,0:T(8,128)(2,1)S(1)}, bf16[3,3,256,256]{3,2,1,0:T(8,128)(2,1)}, u32[]{:S(2)}) copy-start(bf16[3,3,256,256]{3,2,1,0:T(8,128)(2,1)} %param.21) | copy-start | bytes 3538948
  3.0 1.2 %copy-start.1 = (bf16[512,1024]{1,0:T(8,128)(2,1)S(1)}, bf16[512,1024]{1,0:T(8,128)(2,1)}, u32[]{:S(2)}) copy-start(bf16[512,1024]{1,0:T(8,128)(2,1)} %f_out.1) | copy-start | bytes 3145732
  4.2 1.2 %copy-start.2 = (bf16[512,1024]{1,0:T(8,128)(2,1)S(1)}, bf16[512,1024]{1,0:T(8,128)(2,1)}, u32[]{:S(2)}) copy-start(bf16[512,1024]{1,0:T(8,128)(2,1)} %g_out.1) | copy-start | bytes 3145732
  5.4 1.2 %copy-start.3 = (bf16[2048,256]{1,0:T(8,128)(2,1)S(1)}, bf16[2048,256]{1,0:T(8,128)(2,1)}, u32[]{:S(2)}) copy-start(bf16[2048,256]{1,0:T(8,128)(2,1)} %h_proj.1) | copy-start | bytes 3145732
  6.6 0.7 copy-start.4
  7.3 0.7 copy-start.5
  8.0 0.7 copy-start.6
  8.7 0.7 copy-start.7

commit v2 on v1

--- a/solution.py
+++ b/solution.py
@@ -302,16 +302,26 @@
         )
     pl.semaphore_wait(barrier, len(everyone))
 
-    T_CORE, T_X, T_FWD, F_X, F_FWD, G_X, G_FWD = range(7)
-    A_CORE, A_X, A_FWD = 7, 7 + pairs, 7 + 2 * pairs
-    ZQ = 7 + 3 * pairs
+    T_CORE, T_X, T_FWD, F_X, F_Z, F_FWD, G_X, G_FWD = 0, 1, 2, 3, 5, 7, 9, 10
+    A_CORE, A_X, A_FWD = 11, 11 + pairs, 11 + 2 * pairs
+    ZQ = 11 + 3 * pairs
     ZV, ZO = ZQ + seq, ZQ + 2 * seq
     B2 = ZQ + 3 * seq
     HALO = B2 + 4
 
     tok_x = put(T_X, tok, toks.at[2], peers[2])
     tok_core = put(T_CORE, tok, toks.at[1], peers[1])
-    fo_x = put(F_X, f_out.at[own_cols], fo.at[2], peers[2])
+    mine = lax.rem(z, 2)
+    part = cols // 2
+    chunk = part // 2
+
+    def piece(owner, k):
+        return pl.ds(pl.multiple_of(owner * part + k * chunk, chunk), chunk)
+
+    fo_x = []
+    for k in range(2):
+        source = f_out.at[pl.ds(pl.multiple_of(c * cols + mine * part + k * chunk, chunk), chunk)]
+        fo_x.append(put(F_X + k, source, fo.at[2, piece(mine, k)], peers[2]))
 
     block_row = lax.broadcasted_iota(jnp.int32, (rows, 1), 0)
     block_valid = block_row < real
@@ -355,6 +365,15 @@
         att[0, p] = (top / bottom).astype(BF)
         att_x.append(put(A_X + p, att.at[0, p], att.at[2, p], peers[2]))
         att_core.append(put(A_CORE + p, att.at[0, p], att.at[1, p], peers[1]))
+    pair_peer = (s, z + 1 - 2 * mine, x, c)
+    mine_rows = pl.ds(pl.multiple_of(mine * part, part), part)
+    pair_rows = pl.ds(pl.multiple_of((1 - mine) * part, part), part)
+    fo_z = []
+    for k in range(2):
+        fo_x[k].wait_recv()
+        at = piece(mine, k)
+        fo_z.append(put(F_Z + k, fo.at[2, at], fo.at[2, at], pair_peer))
+    fo_fwd = [put(F_FWD, fo.at[2, mine_rows], fo.at[3, mine_rows], peers[1])]
     go_x = put(G_X, g_out.at[own_cols], go.at[2], peers[2])
 
     def gathered(group):
@@ -388,14 +407,14 @@
         ).astype(F32)
         acc[:, at] = base + mm(lhs_near, weight)
 
-    fo_x.wait_recv()
-    fo_fwd = put(F_FWD, fo.at[2], fo.at[3], peers[1])
+    for copy in fo_z:
+        copy.wait_recv()
+    fo_fwd.append(put(F_FWD + 1, fo.at[2, pair_rows], fo.at[3, pair_rows], peers[1]))
     att_fwd = []
     for p in range(pairs):
         att_x[p].wait_recv()
         att_fwd.append(put(A_FWD + p, att.at[2, p], att.at[3, p], peers[1]))
-    fo_fwd.wait_recv()
-    for copy in att_fwd:
+    for copy in fo_fwd + att_fwd:
         copy.wait_recv()
     lhs_far = gathered((2, 3))
 
@@ -562,7 +581,7 @@
     hbm = pl.BlockSpec(memory_space=pl.ANY)
     start = (real - width) // TILE * TILE
     slab = max(up(width), rows - start)
-    copies = 7 + 3 * pairs + 3 * seq + 4 + 2
+    copies = 11 + 3 * pairs + 3 * seq + 4 + 2
     blocks, features = pl.pallas_call(
         functools.partial(scene_kernel, seq, real, width),
         out_shape=(
@@ -603,7 +622,7 @@
             pltpu.SemaphoreType.DMA((8,)),
         ],
         compiler_params=pltpu.CompilerParams(
-            collective_id=0, has_side_effects=True, vmem_limit_bytes=48 * 2**20
+            collective_id=0, has_side_effects=True
         ),
     )(
         flat,
@@ -634,6 +653,7 @@
         and frames == 1
         and heads == 2 * sizes["seq"]
         and sizes["seq"] % 2 == 0
+        and arrays[2].shape[2] // 2 % (4 * TILE) == 0
         and height * width >= up(width)
     )
     if fits:

time: 78.8 us -> 71.7 us (0.910)
  local copies, waits for them, and re-layouts: 10.1 us -> 4.17 us
  Pallas kernels: 67.6 us -> 65.9 us
    unnamed x16 -> x0, local copies, waits for them, and re-layouts: 7.69 us -> none
    pallas_call x1, Pallas kernels: 67.6 us -> 65.9 us  [scene_program(): pl.pallas_call(functools.partial(scene_kernel, seq, real, width), out_sha...]
    reshape x1, local copies, waits for them, and re-layouts: 0.75 us -> 1.69 us  [scene_program(): blocks[:real].reshape(tokens.shape)]
    reshape x1, local copies, waits for them, and re-layouts: 0.64 us -> 1.46 us  [scene_program(): features[:real].reshape(1, height, width, channels)]
where the time goes in v2:
time: 71.7 us; the launch traced here: 71.4 us
  Pallas kernels  65.9 us (92%)
  local copies, waits for them, and re-layouts  4.17 us (6%)
    pallas_call x1, Pallas kernels, scene_program(): pl.pallas_call(functools.partial(scene_kernel, seq, real, width), out_sha...  65.9 us
    reshape x1, local copies, waits for them, and re-layouts, scene_program(): blocks[:real].reshape(tokens.shape)  1.69 us
    reshape x1, local copies, waits for them, and re-layouts, scene_program(): features[:real].reshape(1, height, width, channels)  1.46 us

profile of v2, /device:TPU:0, one launch (start us, length us, event | category | flops | bytes accessed | tf_op | source)
XLA Modules:
  0.0 71.4 jit_solution(4602917196053961597)
XLA Ops:
  0.6 1.0 %reshape.28 = bf16[111,1024]{1,0:T(8,128)(2,1)S(1)} reshape(bf16[1,3,37,1024]{3,2,1,0:T(8,128)(2,1)} %param.11) | data formatting | bytes 454656 | tf_op jit(solution)/shard_map/reshape | solution.py:578
  1.7 0.7 pad_maximum_fusion.tok
  2.4 65.9 %shard_map.122 = (bf16[112,1024]{1,0:T(8,128)(2,1)}, bf16[112,256]{1,0:T(8,128)(2,1)}) custom-call(bf16[112,1024]{1,0:T(8,128)(2,1)} %pad_maximum_fusion.tok, f32[1,1024]{1,0:T(1,128)} %bitcast.11, bf16[3,1024,512]{2,1,0:T(8,128)(2,1)} %f_qkv.1, bf16[512,1024]{1,0:T(8,128)(2,1)} %f_out.1, f32[1,1024]{1,0:T(1,128)} %bitcast.12, bf16[3,1024,512]{2,1,0:T(8,128)(2,1)} %g_qkv.1, ...), custom_call_target="tpu_custom_call" | custom-call | tf_op jit(solution)/shard_map/pallas_call | solution.py:585
  68.3 1.7 %reshape.34 = bf16[1,3,37,1024]{3,2,1,0:T(8,128)(2,1)} reshape(bf16[111,1024]{1,0:T(8,128)(2,1)} %bitcast.8) | data formatting | bytes 454656 | tf_op jit(solution)/shard_map/reshape | solution.py:641
  70.0 1.5 %reshape.35 = bf16[1,3,37,256]{3,2,1,0:T(8,128)(2,1)} reshape(bf16[111,256]{1,0:T(8,128)(2,1)} %bitcast.9) | data formatting | bytes 113664 | tf_op jit(solution)/shard_map/reshape | solution.py:642
  (1 shorter events, 0.0 us)
